TPU v7x, 32 devices: a whole 2x2x4 slice. The times are simulated.
32 devices in a mesh: dp: 8 (over y, x, core), tensor: 4 (over z).
Axes of the slice: x: 2, y: 2, z: 4, core: 2. Of those that a mesh axis runs over, the one named last changes fastest.
Arguments:
- tokens: bfloat16 [16384, 1024], P(('dp', 'tensor')), may hold values from -6 to 6
- norm_gains: float32 [2, 1024], replicated, may hold values from 0.5 to 1.5
- attn_qkv: bfloat16 [3, 1024, 1024], P(None, None, 'tensor'), may hold values from -0.09375 to 0.09375
- attn_out: bfloat16 [1024, 1024], P('tensor'), may hold values from -1.5 to 1.5
- ffn_in: bfloat16 [2, 1024, 2816], P(None, None, 'tensor'), may hold values from -0.1875 to 0.1875
- ffn_out: bfloat16 [2816, 1024], P('tensor'), may hold values from -0.109375 to 0.109375
- position_tables: float32 [3, 32, 16], P(None, None, 'tensor'), may hold values from -5 to 5
- page_counts: int32 [16], P('dp'), may hold values from 64 to 1024, as said below
- layout_cells: int32 [2, 16384], P(None, 'dp'), may hold values from 0 to 63
- cotangent: bfloat16 [16384, 1024], P(('dp', 'tensor')), may hold values from -6 to 6
Outputs:
- layer_out: bfloat16 [16384, 1024], P(('dp', 'tensor'))
- tokens_grad: float32 [16384, 1024], P(('dp', 'tensor'))
- gains_grad: float32 [2, 1024], P(None, ('dp', 'tensor'))
- qkv_grad: float32 [3, 1024, 1024], P(None, 'dp', 'tensor')
- out_grad: float32 [1024, 1024], P('tensor', 'dp')
- inner_grad: float32 [2, 1024, 2816], P(None, 'dp', 'tensor')
- outer_grad: float32 [2816, 1024], P('tensor', 'dp')
- tables_grad: float32 [3, 32, 16], P(None, 'dp', 'tensor')
Inputs may be any that keep to these rules, and one draw needn't show every extreme that they name: `page_counts`: true token count of each page; a page's tokens at or past it are padding that no query attends to. Some page is full and some page has the least count in every draw.
All inputs are finite; a program needn't handle non-finite values.
Results may differ from a plain program's by a relative error of at most 0.022.
Values may be sent and summed in bfloat16 or wider, within the bound.
A program may use at most 256 MiB of HBM per device.

v0:
```python
import math
import jax
import jax.numpy as jnp
import numpy as np
from jax import lax
from jax.sharding import PartitionSpec as P

HEAD_DIM = 64
BUCKETS = 32
REL_REACH = 128
CELLS = 64
PAGE_LEN = 1024
HIGHEST_PRECISION = lax.Precision.HIGHEST
TABLE_PRECISION = lax.Precision.HIGH
NORM_EPSILON = 1e-06
MASK_VALUE = -1e30


def bucket_table(offsets, bucket_total, max_reach):
    half_total = bucket_total // 2
    exact_limit = half_total // 2
    distance = np.abs(offsets).astype(np.int32)
    upper_side = (offsets > 0).astype(np.int32) * half_total
    safe_dist = np.maximum(distance, 1).astype(np.float32)
    ratio = np.log(safe_dist / np.float32(exact_limit)) / np.float32(
        math.log(max_reach / exact_limit)
    )
    far_bucket = exact_limit + np.floor(ratio * np.float32(half_total - exact_limit)).astype(
        np.int32
    )
    far_bucket = np.minimum(far_bucket, half_total - 1)
    return (upper_side + np.where(distance < exact_limit, distance, far_bucket)).astype(np.int32)


def offset_onehot(length):
    offsets = np.arange(2 * length - 1) - (length - 1)
    buckets = bucket_table(offsets, BUCKETS, REL_REACH)
    return jnp.asarray((buckets[:, None] == np.arange(BUCKETS)[None, :]).astype(np.float32))


def layout_onehot():
    cell_range = np.arange(CELLS)
    buckets = bucket_table(cell_range[None, :] - cell_range[:, None], BUCKETS, CELLS)
    return jnp.asarray(
        (buckets.reshape(-1)[:, None] == np.arange(BUCKETS)[None, :]).astype(np.float32)
    )


def gelu_tanh(values):
    return jax.nn.gelu(values, approximate=True)


def relative_bias(table_rows, length):
    values = jnp.dot(offset_onehot(length), table_rows, precision=HIGHEST_PRECISION).T
    heads_dev = values.shape[0]
    padded = jnp.pad(values, ((0, 0), (0, 1)))
    tiled = jnp.tile(padded, (1, length))
    skewed = tiled[:, : length * (2 * length - 1)].reshape(heads_dev, length, 2 * length - 1)
    return skewed[:, :, length - 1 :]


def relative_sums(dscore, length):
    heads_dev = dscore.shape[0]
    placed = jnp.pad(dscore, ((0, 0), (0, 0), (length - 1, 0)))
    flat = jnp.pad(placed.reshape(heads_dev, length * (2 * length - 1)), ((0, 0), (0, length)))
    return jnp.sum(flat.reshape(heads_dev, length, 2 * length), axis=1)[:, : 2 * length - 1]


def layout_values(tables):
    values = jnp.einsum("mn,snh->shm", layout_onehot(), tables[1:], precision=HIGHEST_PRECISION)
    return values.reshape(2, tables.shape[2], CELLS, CELLS)


def cell_onehots(page_cells):
    onehot = (page_cells[:, :, None] == jnp.arange(CELLS)[None, None, :]).astype(jnp.float32)
    length = page_cells.shape[1]
    joined = onehot.transpose(1, 0, 2).reshape(length, 2 * CELLS)
    return (onehot, joined)


def layout_bias(page_cells, lay_vals):
    onehot, joined = cell_onehots(page_cells)
    length = page_cells.shape[1]
    heads_dev = lay_vals.shape[1]
    rows_side = jnp.einsum("sia,shab->hisb", onehot, lay_vals, precision=TABLE_PRECISION)
    rows_side = rows_side.reshape(heads_dev, length, 2 * CELLS)
    return jnp.einsum("hic,jc->hij", rows_side, joined, precision=TABLE_PRECISION)


def layout_sums(dscore, page_cells):
    onehot, joined = cell_onehots(page_cells)
    length = page_cells.shape[1]
    heads_dev = dscore.shape[0]
    partial_rows = jnp.einsum("hij,jc->hic", dscore, joined, precision=TABLE_PRECISION)
    partial_rows = partial_rows.reshape(heads_dev, length, 2, CELLS)
    return jnp.einsum("sia,hisb->shab", onehot, partial_rows, precision=TABLE_PRECISION)


def page_scores(query, key_rows, count, page_cells, rel_bias, lay_vals):
    length = query.shape[0]
    scores = jnp.einsum("ihd,jhd->hij", query, key_rows, preferred_element_type=jnp.float32)
    scores = scores + rel_bias + layout_bias(page_cells, lay_vals)
    valid = jnp.arange(length) < count
    return jnp.where(valid[None, None, :], scores, MASK_VALUE)


def attend(projected, page_counts, layout_cells, rel_bias, lay_vals):
    total_rows = projected.shape[1]
    pages = page_counts.shape[0]
    length = total_rows // pages
    heads_dev = projected.shape[2] // HEAD_DIM
    split = projected.reshape(3, pages, length, heads_dev, HEAD_DIM)
    cells_pages = layout_cells.reshape(2, pages, length).transpose(1, 0, 2)

    def one_page(items):
        query, key_rows, value_rows, count, page_cells = items
        scores = page_scores(query, key_rows, count, page_cells, rel_bias, lay_vals)
        log_total = jax.nn.logsumexp(scores, axis=2)
        prob_low = jnp.exp(scores - log_total[:, :, None]).astype(jnp.bfloat16)
        context = jnp.einsum(
            "hij,jhd->ihd", prob_low, value_rows, preferred_element_type=jnp.float32
        )
        return (context.astype(jnp.bfloat16).reshape(length, heads_dev * HEAD_DIM), log_total)

    context, log_totals = lax.map(
        one_page, (split[0], split[1], split[2], page_counts, cells_pages)
    )
    return (context.reshape(total_rows, heads_dev * HEAD_DIM), log_totals)


def attend_back(projected, grad_context, log_totals, page_counts, layout_cells, rel_bias, lay_vals):
    total_rows = projected.shape[1]
    pages = page_counts.shape[0]
    length = total_rows // pages
    heads_dev = projected.shape[2] // HEAD_DIM
    split = projected.reshape(3, pages, length, heads_dev, HEAD_DIM)
    grad_split = grad_context.reshape(pages, length, heads_dev, HEAD_DIM)
    cells_pages = layout_cells.reshape(2, pages, length).transpose(1, 0, 2)

    def page_step(carry, items):
        rel_acc, lay_acc = carry
        query, key_rows, value_rows, grad_ctx, page_lse, count, page_cells = items
        scores = page_scores(query, key_rows, count, page_cells, rel_bias, lay_vals)
        prob = jnp.exp(scores - page_lse[:, :, None])
        grad_prob = jnp.einsum(
            "ihd,jhd->hij", grad_ctx, value_rows, preferred_element_type=jnp.float32
        )
        delta = jnp.sum(grad_prob * prob, axis=2, keepdims=True)
        dscore = prob * (grad_prob - delta)
        rel_acc = rel_acc + relative_sums(dscore, length)
        lay_acc = lay_acc + layout_sums(dscore, page_cells)
        score_low = dscore.astype(jnp.bfloat16)
        grad_query = jnp.einsum(
            "hij,jhd->ihd", score_low, key_rows, preferred_element_type=jnp.float32
        ).astype(jnp.bfloat16)
        grad_key = jnp.einsum(
            "hij,ihd->jhd", score_low, query, preferred_element_type=jnp.float32
        ).astype(jnp.bfloat16)
        grad_value = jnp.einsum(
            "hij,ihd->jhd", prob.astype(jnp.bfloat16), grad_ctx, preferred_element_type=jnp.float32
        ).astype(jnp.bfloat16)
        stacked = jnp.stack([grad_query, grad_key, grad_value]).reshape(
            3, length, heads_dev * HEAD_DIM
        )
        return ((rel_acc, lay_acc), stacked)

    init_sums = (
        jnp.zeros((heads_dev, 2 * length - 1), jnp.float32),
        jnp.zeros((2, heads_dev, CELLS, CELLS), jnp.float32),
    )
    (rel_acc, lay_acc), grads = lax.scan(
        page_step,
        init_sums,
        (split[0], split[1], split[2], grad_split, log_totals, page_counts, cells_pages),
    )
    grad_proj = grads.transpose(1, 0, 2, 3).reshape(3, total_rows, heads_dev * HEAD_DIM)
    rel_grad = jnp.dot(offset_onehot(length).T, rel_acc.T, precision=HIGHEST_PRECISION)
    lay_grad = jnp.einsum(
        "shm,mn->snh",
        lay_acc.reshape(2, heads_dev, CELLS * CELLS),
        layout_onehot(),
        precision=HIGHEST_PRECISION,
    )
    return (grad_proj, jnp.concatenate([rel_grad[None], lay_grad], axis=0))


def norm_back(rows, scale, gain, grad_normed):
    weighted = grad_normed * gain
    return scale * weighted - rows * scale**3 * jnp.mean(rows * weighted, axis=1, keepdims=True)


def forward_core(
    token_rows,
    norm_gains,
    attn_qkv,
    attn_out,
    ffn_in,
    page_counts,
    layout_cells,
    rel_bias,
    lay_vals,
):
    scale_one = lax.rsqrt(jnp.mean(token_rows * token_rows, axis=1, keepdims=True) + NORM_EPSILON)
    normed_one = (token_rows * scale_one * norm_gains[0]).astype(jnp.bfloat16)
    gathered_one = lax.all_gather(normed_one, "tensor", axis=0, tiled=True)
    projected = jnp.einsum(
        "td,cdk->ctk", gathered_one, attn_qkv, preferred_element_type=jnp.float32
    ).astype(jnp.bfloat16)
    context, log_totals = attend(projected, page_counts, layout_cells, rel_bias, lay_vals)
    attn_total = lax.psum_scatter(
        jnp.dot(context, attn_out, preferred_element_type=jnp.float32)
        .astype(jnp.bfloat16)
        .astype(jnp.float32)
        .astype(jnp.bfloat16),
        "tensor",
        scatter_dimension=0,
        tiled=True,
    ).astype(jnp.float32)
    resid = token_rows + attn_total
    scale_two = lax.rsqrt(jnp.mean(resid * resid, axis=1, keepdims=True) + NORM_EPSILON)
    normed_two = (resid * scale_two * norm_gains[1]).astype(jnp.bfloat16)
    gathered_two = lax.all_gather(normed_two, "tensor", axis=0, tiled=True)
    gate_up = jnp.einsum("td,cdf->ctf", gathered_two, ffn_in, preferred_element_type=jnp.float32)
    hidden = (gelu_tanh(gate_up[0]) * gate_up[1]).astype(jnp.bfloat16)
    return (
        scale_one,
        gathered_one,
        projected,
        context,
        log_totals,
        resid,
        scale_two,
        gathered_two,
        gate_up,
        hidden,
    )


def body(
    tokens,
    norm_gains,
    attn_qkv,
    attn_out,
    ffn_in,
    ffn_out,
    position_tables,
    page_counts,
    layout_cells,
    cotangent,
):
    token_rows = tokens.astype(jnp.float32)
    rel_bias = relative_bias(position_tables[0], PAGE_LEN)
    lay_vals = layout_values(position_tables)
    first = forward_core(
        token_rows,
        norm_gains,
        attn_qkv,
        attn_out,
        ffn_in,
        page_counts,
        layout_cells,
        rel_bias,
        lay_vals,
    )
    first_hidden = first[9]
    rows_part = first_hidden
    ffn_total = lax.psum_scatter(
        jnp.dot(rows_part, ffn_out, preferred_element_type=jnp.float32)
        .astype(jnp.bfloat16)
        .astype(jnp.float32)
        .astype(jnp.bfloat16),
        "tensor",
        scatter_dimension=0,
        tiled=True,
    ).astype(jnp.float32)
    layer_out = (first[5] + ffn_total).astype(jnp.bfloat16)
    cot_rows = lax.all_gather(cotangent, "tensor", axis=0, tiled=True)
    again_rows, cot_rows = lax.optimization_barrier((token_rows, cot_rows))
    saved = forward_core(
        again_rows,
        norm_gains,
        attn_qkv,
        attn_out,
        ffn_in,
        page_counts,
        layout_cells,
        rel_bias,
        lay_vals,
    )
    (
        scale_one,
        gathered_one,
        projected,
        context,
        log_totals,
        resid,
        scale_two,
        gathered_two,
        gate_up,
        hidden,
    ) = saved
    grad_hidden = jnp.einsum("td,fd->tf", cot_rows, ffn_out, preferred_element_type=jnp.float32)
    outer_grad = jnp.einsum("tf,td->fd", hidden, cot_rows, preferred_element_type=jnp.float32)
    gelu_value, gelu_back = jax.vjp(gelu_tanh, gate_up[0])
    grad_gate = gelu_back(grad_hidden * gate_up[1])[0].astype(jnp.bfloat16)
    grad_up = (grad_hidden * gelu_value).astype(jnp.bfloat16)
    grad_gate_up = jnp.stack([grad_gate, grad_up])
    inner_grad = jnp.einsum(
        "td,ctf->cdf", gathered_two, grad_gate_up, preferred_element_type=jnp.float32
    )
    rows_part = grad_gate_up
    grad_normed_two = lax.psum_scatter(
        jnp.einsum("ctf,cdf->td", rows_part, ffn_in, preferred_element_type=jnp.float32)
        .astype(jnp.bfloat16)
        .astype(jnp.float32)
        .astype(jnp.bfloat16),
        "tensor",
        scatter_dimension=0,
        tiled=True,
    ).astype(jnp.float32)
    grad_resid = cotangent.astype(jnp.float32) + norm_back(
        resid, scale_two, norm_gains[1], grad_normed_two
    )
    gain_two = jnp.sum(grad_normed_two * resid * scale_two, axis=0)
    resid_rows = lax.all_gather(grad_resid.astype(jnp.bfloat16), "tensor", axis=0, tiled=True)
    out_grad = jnp.einsum("tk,td->kd", context, resid_rows, preferred_element_type=jnp.float32)
    grad_context = jnp.einsum(
        "td,kd->tk", resid_rows, attn_out, preferred_element_type=jnp.float32
    ).astype(jnp.bfloat16)
    grad_proj, tables_grad = attend_back(
        projected, grad_context, log_totals, page_counts, layout_cells, rel_bias, lay_vals
    )
    qkv_grad = jnp.einsum(
        "td,ctk->cdk", gathered_one, grad_proj, preferred_element_type=jnp.float32
    )
    rows_part = grad_proj
    grad_normed_one = lax.psum_scatter(
        jnp.einsum("ctk,cdk->td", rows_part, attn_qkv, preferred_element_type=jnp.float32)
        .astype(jnp.bfloat16)
        .astype(jnp.float32)
        .astype(jnp.bfloat16),
        "tensor",
        scatter_dimension=0,
        tiled=True,
    ).astype(jnp.float32)
    tokens_grad = grad_resid + norm_back(token_rows, scale_one, norm_gains[0], grad_normed_one)
    gain_one = jnp.sum(grad_normed_one * token_rows * scale_one, axis=0)
    gains_grad = lax.psum_scatter(
        jnp.stack([gain_one, gain_two]), ("dp", "tensor"), scatter_dimension=1, tiled=True
    )
    qkv_summed, inner_summed, out_summed, outer_summed, tables_summed = (
        lax.psum_scatter(
            qkv_grad.astype(jnp.bfloat16), "dp", scatter_dimension=1, tiled=True
        ).astype(jnp.float32),
        lax.psum_scatter(
            inner_grad.astype(jnp.bfloat16), "dp", scatter_dimension=1, tiled=True
        ).astype(jnp.float32),
        lax.psum_scatter(
            out_grad.astype(jnp.bfloat16), "dp", scatter_dimension=1, tiled=True
        ).astype(jnp.float32),
        lax.psum_scatter(
            outer_grad.astype(jnp.bfloat16), "dp", scatter_dimension=1, tiled=True
        ).astype(jnp.float32),
        lax.psum_scatter(
            tables_grad.astype(jnp.bfloat16), "dp", scatter_dimension=1, tiled=True
        ).astype(jnp.float32),
    )
    return (
        layer_out,
        tokens_grad,
        gains_grad,
        qkv_summed,
        out_summed,
        inner_summed,
        outer_summed,
        tables_summed,
    )


def solution(mesh):
    return jax.shard_map(
        body,
        mesh=mesh,
        in_specs=(
            P(("dp", "tensor"), None),
            P(),
            P(None, None, "tensor"),
            P("tensor", None),
            P(None, None, "tensor"),
            P("tensor", None),
            P(None, None, "tensor"),
            P("dp"),
            P(None, "dp"),
            P(("dp", "tensor"), None),
        ),
        out_specs=(
            P(("dp", "tensor"), None),
            P(("dp", "tensor"), None),
            P(None, ("dp", "tensor")),
            P(None, "dp", "tensor"),
            P("tensor", "dp"),
            P(None, "dp", "tensor"),
            P("tensor", "dp"),
            P(None, "dp", "tensor"),
        ),
        check_vma=False,
    )
```

profile of v0, /device:TPU:0, one launch (start us, length us, event | category | flops | bytes accessed | tf_op | source)
XLA Modules:
  0.0 2264.0 jit_solution(10170065226509743736)
XLA Ops:
  11.5 81.6 %all-gather.11.cloned.1.call-done = bf16[2048,1024]{1,0:T(8,128)(2,1)} async-done(((bf16[512,1024]{1,0:T(8,128)(2,1)}), bf16[2048,1024]{1,0:T(8,128)(2,1)}) %all-gather.11.cloned.1.call-update) | async-done | bytes 4194320 | tf_op jit(solution)/shard_map/all_gather | solution.py:277
  113.7 38.0 %copy.157 = f32[1,4,1024,2048]{3,1,2,0:T(4,128)} copy(f32[1,4,1024,2048]{3,2,1,0:T(8,128)} %broadcast_bitcast_fusion) | data formatting | bytes 67108864
  151.7 23.8 %slice.90 = f32[4,2096128]{1,0:T(4,128)} slice(f32[4,2097152]{1,0:T(4,128)} %bitcast.428), slice={[0:4], [0:2096128]} | slice | bytes 67076096 | tf_op jit(solution)/shard_map/slice | solution.py:58
  175.5 94.2 %reshape.284 = f32[8384512]{0:T(1024)} reshape(f32[4,2096128]{1,0:T(4,128)} %slice.90) | data formatting | bytes 67076096
  269.7 49.8 %reshape.234 = f32[4,1024,2047]{2,1,0:T(8,128)} reshape(f32[8384512]{0:T(1024)} %reshape.284) | data formatting | bytes 67076096 | tf_op jit(solution)/shard_map/reshape | solution.py:58
  383.8 108.1 %while.40 = (s32[]{:T(128)}, bf16[2,1024,256]{2,1,0:T(8,128)(2,1)}, f32[2,4,1024]{2,1,0:T(4,128)}, bf16[2,1024,4,64]{1,3,2,0:T(8,128)(2,1)}, s32[2]{0:T(128)}, /...) while((s32[]{:T(128)}, bf16[2,1024,256]{2,1,0:T(8,128)(2,1)}, ...), condition=%wide.region_12.13_spmd, body=%wide.region_9.12_spmd.sunk | while | flops 4530406400 | bytes 113618096 | solution.py:125
  497.0 75.1 %reduce-scatter.26.cloned.1.call-done = bf16[512,1024]{1,0:T(8,128)(2,1)} async-done(((bf16[2048,1024]{1,0:T(8,128)(2,1)}), bf16[512,1024]{1,0:T(8,128)(2,1)}) %reduce-scatter.26.cloned.1.call-update) | async-done | bytes 1048592 | tf_op jit(solution)/shard_map/reduce_scatter | solution.py:210
  577.3 81.4 %all-gather.15.cloned.1.call-done = bf16[2048,1024]{1,0:T(8,128)(2,1)} async-done(((bf16[512,1024]{1,0:T(8,128)(2,1)}), bf16[2048,1024]{1,0:T(8,128)(2,1)}) %all-gather.15.cloned.1.call-update) | async-done | bytes 4194320 | tf_op jit(solution)/shard_map/all_gather | solution.py:222
  685.4 75.4 %reduce-scatter.28.cloned.1.call-done = bf16[512,1024]{1,0:T(8,128)(2,1)} async-done(((bf16[2048,1024]{1,0:T(8,128)(2,1)}), bf16[512,1024]{1,0:T(8,128)(2,1)}) %reduce-scatter.28.cloned.1.call-update) | async-done | bytes 1048592 | tf_op jit(solution)/shard_map/reduce_scatter | solution.py:312
  768.8 80.9 %all-gather.17.cloned.1.call-done = bf16[2048,1024]{1,0:T(8,128)(2,1)} async-done(((bf16[512,1024]{1,0:T(8,128)(2,1)}), bf16[2048,1024]{1,0:T(8,128)(2,1)}) %all-gather.17.cloned.1.call-update) | async-done | bytes 4194320 | tf_op jit(solution)/shard_map/all_gather | solution.py:325
  862.8 531.5 %while.41 = (s32[]{:T(128)}, f32[4,2047]{1,0:T(4,128)}, f32[2,4,64,64]{2,3,1,0:T(8,128)S(1)}, bf16[2,3,1024,256]{3,2,0,1:T(8,128)(2,1)}, s32[2]{0:T(128)}, /*ind...) while((s32[]{:T(128)}, f32[4,2047]{1,0:T(4,128)}, ...), condition=%wide.region_20.21_spmd.clone, body=%wide.region_17.20_spmd.clone.sunk | while | flops 9586938880 | bytes 645969984 | solution.py:171
  995.9 46.4 %reshape.288 = f32[8384512]{0:T(1024)} reshape(f32[4,1024,2047]{2,1,0:T(8,128)} %pad.19.clone.2) | data formatting | bytes 67076096 | tf_op jit(solution)/shard_map/while
  1042.4 40.4 %reshape.289 = f32[4,2096128]{1,0:T(4,128)} reshape(f32[8384512]{0:T(1024)} %reshape.288) | data formatting | bytes 67076096 | tf_op jit(solution)/shard_map/while/body/eval_jaxpr/reshape | solution.py:65
  1258.6 46.2 %reshape.288 = f32[8384512]{0:T(1024)} reshape(f32[4,1024,2047]{2,1,0:T(8,128)} %pad.19.clone.2) | data formatting | bytes 67076096 | tf_op jit(solution)/shard_map/while
  1304.8 40.4 %reshape.289 = f32[4,2096128]{1,0:T(4,128)} reshape(f32[8384512]{0:T(1024)} %reshape.288) | data formatting | bytes 67076096 | tf_op jit(solution)/shard_map/while/body/eval_jaxpr/reshape | solution.py:65
  1402.4 75.4 %reduce-scatter.30.cloned.1.call-done = bf16[512,1024]{1,0:T(8,128)(2,1)} async-done(((bf16[2048,1024]{1,0:T(8,128)(2,1)}), bf16[512,1024]{1,0:T(8,128)(2,1)}) %reduce-scatter.30.cloned.1.call-update) | async-done | bytes 1048592 | tf_op jit(solution)/shard_map/reduce_scatter | solution.py:337
  1485.7 81.4 %all-gather.7.cloned.1.call-done = bf16[2048,1024]{1,0:T(8,128)(2,1)} async-done(((bf16[512,1024]{1,0:T(8,128)(2,1)}), bf16[2048,1024]{1,0:T(8,128)(2,1)}) %all-gather.7.cloned.1.call-update) | async-done | bytes 4194320 | tf_op jit(solution)/shard_map/all_gather | solution.py:205
  1601.7 106.5 %while.39 = (s32[]{:T(128)}, bf16[2,1024,256]{2,1,0:T(8,128)(2,1)}, bf16[2,1024,4,64]{1,3,2,0:T(8,128)(2,1)}, s32[2]{0:T(128)}, bf16[2,1024,4,64]{1,3,2,0:T(8,12...) while((s32[]{:T(128)}, bf16[2,1024,256]{2,1,0:T(8,128)(2,1)}, ...), condition=%wide.region_4.5_spmd, body=%wide.region_1.4_spmd.sunk | while | flops 4530390016 | bytes 113568936 | solution.py:125
  1713.4 75.0 %reduce-scatter.22.cloned.1.call-done = bf16[512,1024]{1,0:T(8,128)(2,1)} async-done(((bf16[2048,1024]{1,0:T(8,128)(2,1)}), bf16[512,1024]{1,0:T(8,128)(2,1)}) %reduce-scatter.22.cloned.1.call-update) | async-done | bytes 1048592 | tf_op jit(solution)/shard_map/reduce_scatter | solution.py:210
  1890.3 24.7 %reduce-scatter.40.cloned.1.call-done = bf16[128,704]{1,0:T(8,128)(2,1)} async-done(((bf16[1024,704]{1,0:T(8,128)(2,1)}), bf16[128,704]{1,0:T(8,128)(2,1)}) %reduce-scatter.40.cloned.1.call-update) | async-done | bytes 180240
  1916.8 46.3 %reduce-scatter.38.cloned.1.call-done = bf16[128,1408]{1,0:T(8,128)(2,1)} async-done(((bf16[1024,1408]{1,0:T(8,128)(2,1)}), bf16[128,1408]{1,0:T(8,128)(2,1)}) %reduce-scatter.38.cloned.1.call-update) | async-done | bytes 360464
  2002.3 40.0 %reduce-scatter.34.cloned.1.call-done = bf16[128,768]{1,0:T(8,128)(2,1)} async-done(((bf16[1024,768]{1,0:T(8,128)(2,1)}), bf16[128,768]{1,0:T(8,128)(2,1)}) %reduce-scatter.34.cloned.1.call-update) | async-done | bytes 196624
  2044.4 134.1 %reduce-scatter.32.cloned.1.call-done = f32[32,2]{1,0:T(8,128)} async-done(((f32[1024,2]{1,0:T(8,128)}), f32[32,2]{1,0:T(8,128)}) %reduce-scatter.32.cloned.1.call-update) | async-done | bytes 272
  2179.8 74.0 %reduce-scatter.24.cloned.1.call-done = bf16[512,1024]{1,0:T(8,128)(2,1)} async-done(((bf16[2048,1024]{1,0:T(8,128)(2,1)}), bf16[512,1024]{1,0:T(8,128)(2,1)}) %reduce-scatter.24.cloned.1.call-update) | async-done | bytes 1048592 | tf_op jit(solution)/shard_map/reduce_scatter | solution.py:267
  (322 shorter events, 916.7 us)
Async XLA Ops:
  7.2 651.5 %copy-start = (bf16[2,1024,704]{1,2,0:T(8,128)(2,1)S(1)}, bf16[2,1024,704]{1,2,0:T(8,128)(2,1)}, u32[]{:S(2)}) copy-start(bf16[2,1024,704]{1,2,0:T(8,128)(2,1)} %param.24) | copy-start | bytes 8650756
  7.2 85.9 %all-gather.11.cloned.1.call-start = ((), (), s32[]{:S(2)}) async-start(), calls=%async_computation.14 | async-start | bytes 5242880 | tf_op jit(solution)/shard_map/all_gather | solution.py:277
  7.9 91.1 %copy-start.16 = (f32[4096,32,1]{0,1,2:T(8,128)S(1)}, f32[4096,32,1]{0,1,2:T(8,128)}, u32[]{:S(2)}) copy-start(f32[4096,32,1]{0,1,2:T(8,128)} %constant.127) | copy-start | bytes 1572868
  7.9 91.1 %copy-start.29 = (f32[3,32,4]{1,2,0:T(4,128)S(1)}, f32[3,32,4]{1,2,0:T(4,128)}, u32[]{:S(2)}) copy-start(f32[3,32,4]{1,2,0:T(4,128)} %param.26) | copy-start | bytes 4612
  7.9 341.4 %all-gather.13.cloned.1.call-start = ((), (), s32[]{:S(2)}) async-start(), calls=%async_computation.15 | async-start | bytes 5242880 | tf_op jit(solution)/shard_map/all_gather | solution.py:205
  11.5 87.5 %copy-start.21 = (f32[1,1024]{1,0:T(1,128)}, f32[1,1024]{1,0:T(1,128)S(1)}, u32[]{:S(2)}) copy-start(f32[1,1024]{1,0:T(1,128)S(1)} %get-tuple-element.537) | copy-start | bytes 12292
  98.9 473.2 %reduce-scatter.26.cloned.1.call-start = ((), (), s32[]{:S(2)}) async-start(), calls=%async_computation.16 | async-start | bytes 5242880 | tf_op jit(solution)/shard_map/reduce_scatter | solution.py:210
  496.7 77.8 %copy-start.19 = (f32[1,1024]{1,0:T(1,128)S(1)}, f32[1,1024]{1,0:T(1,128)}, u32[]{:S(2)}) copy-start(f32[1,1024]{1,0:T(1,128)} %get-tuple-element.536) | copy-start | bytes 12292
  496.7 162.0 %all-gather.15.cloned.1.call-start = ((), (), s32[]{:S(2)}) async-start(), calls=%async_computation.17 | async-start | bytes 5242880 | tf_op jit(solution)/shard_map/all_gather | solution.py:222
  577.3 183.6 %reduce-scatter.28.cloned.1.call-start = ((), (), s32[]{:S(2)}) async-start(), calls=%async_computation.18 | async-start | bytes 5242880 | tf_op jit(solution)/shard_map/reduce_scatter | solution.py:312
  685.4 164.3 %all-gather.17.cloned.1.call-start = ((), (), s32[]{:S(2)}) async-start(), calls=%async_computation.19 | async-start | bytes 5242880 | tf_op jit(solution)/shard_map/all_gather | solution.py:325
  768.3 709.5 %reduce-scatter.30.cloned.1.call-start = ((), (), s32[]{:S(2)}) async-start(), calls=%async_computation.20 | async-start | bytes 5242880 | tf_op jit(solution)/shard_map/reduce_scatter | solution.py:337
  1402.3 78.6 %copy-start.28 = (f32[512]{0:T(512)S(1)}, f32[512]{0:T(512)}, u32[]{:S(2)}) copy-start(f32[512]{0:T(512)} %get-tuple-element.538) | copy-start | bytes 6148
  1402.4 164.7 %all-gather.7.cloned.1.call-start = ((), (), s32[]{:S(2)}) async-start(), calls=%async_computation.10 | async-start | bytes 5242880 | tf_op jit(solution)/shard_map/all_gather | solution.py:205
  1485.6 302.7 %reduce-scatter.22.cloned.1.call-start = ((), (), s32[]{:S(2)}) async-start(), calls=%async_computation.11 | async-start | bytes 5242880 | tf_op jit(solution)/shard_map/reduce_scatter | solution.py:210
  1712.9 77.4 %copy-start.20 = (f32[1,1024]{1,0:T(1,128)S(1)}, f32[1,1024]{1,0:T(1,128)}, u32[]{:S(2)}) copy-start(f32[1,1024]{1,0:T(1,128)} %get-tuple-element.536) | copy-start | bytes 12292
  1712.9 161.7 %all-gather.9.cloned.1.call-start = ((), (), s32[]{:S(2)}) async-start(), calls=%async_computation.12 | async-start | bytes 5242880 | tf_op jit(solution)/shard_map/all_gather | solution.py:222
  1793.2 121.8 %reduce-scatter.40.cloned.1.call-start = ((), (), s32[]{:S(2)}) async-start(), calls=%async_computation.25 | async-start | bytes 1769472
  1806.4 156.7 %reduce-scatter.38.cloned.1.call-start = ((), (), s32[]{:S(2)}) async-start(), calls=%async_computation.24 | async-start | bytes 3244032
  1833.4 167.3 %reduce-scatter.36.cloned.1.call-start = ((), (), s32[]{:S(2)}) async-start(), calls=%async_computation.23 | async-start | bytes 589824
  1838.3 204.0 %reduce-scatter.34.cloned.1.call-start = ((), (), s32[]{:S(2)}) async-start(), calls=%async_computation.22 | async-start | bytes 1769472
  1853.6 324.9 %reduce-scatter.32.cloned.1.call-start = ((), (), s32[]{:S(2)}) async-start(), calls=%async_computation.21 | async-start | bytes 540672
  1854.8 399.1 %reduce-scatter.24.cloned.1.call-start = ((), (), s32[]{:S(2)}) async-start(), calls=%async_computation.13 | async-start | bytes 5242880 | tf_op jit(solution)/shard_map/reduce_scatter | solution.py:267
  1888.4 79.1 %copy-start.14 = (f32[2,4,64,64]{2,3,1,0:T(8,128)S(1)}, f32[2,4,64,64]{2,3,1,0:T(8,128)}, u32[]{:S(2)}) copy-start(f32[2,4,64,64]{2,3,1,0:T(8,128)} %copy-done.13) | copy-start | bytes 393220
  (40 other events, 450.3 us)
Sparse Core Ops, SparseCore 0:
  9.6 83.4 all-gather.10
  99.0 79.2 all-gather.12
  496.8 75.2 reduce-scatter.25
  577.4 81.2 all-gather.14
  685.5 75.2 reduce-scatter.27
  768.4 81.2 all-gather.16
  1402.5 75.2 reduce-scatter.29
  1485.7 81.2 all-gather.6
  1713.0 75.2 reduce-scatter.21
  1793.4 81.2 all-gather.8
  1878.0 36.9 reduce-scatter.39
  1918.2 44.8 reduce-scatter.37
  1966.5 34.1 reduce-scatter.35
  2003.8 38.4 reduce-scatter.33
  2044.4 134.0 reduce-scatter.31
  2180.7 73.0 reduce-scatter.23
where the time goes:
time: 2270 us; the launch traced here: 2260 us
  waiting for transfers between devices  982 us (43%)
  local copies, waits for them, and re-layouts  699 us (31%)
  matrix products  404 us (18%)
  other arithmetic  142 us (6%)
    unnamed x21, waiting for transfers between devices  262 us
    unnamed x73, local copies, waits for them, and re-layouts  189 us
    reduce_scatter x2, waiting for transfers between devices, forward_core(): lax.psum_scatter(jnp.dot(context, attn_out, preferred_element_type=jnp.fl...  150 us
    while x48, local copies, waits for them, and re-layouts  135 us
    dot_general x6, matrix products, page_scores(): jnp.einsum('ihd,jhd->hij', query, key_rows, preferred_element_type=jnp.fl...  116 us
    all_gather x2, waiting for transfers between devices, forward_core(): gathered_two = lax.all_gather(normed_two, 'tensor', axis=0, tiled=True)  101 us
    all_gather x1, waiting for transfers between devices, body(): cot_rows = lax.all_gather(cotangent, 'tensor', axis=0, tiled=True)  81.6 us
    all_gather x2, waiting for transfers between devices, forward_core(): gathered_one = lax.all_gather(normed_one, 'tensor', axis=0, tiled=True)  81.4 us
  transfers between devices with their start and end apart: 16, of which 15 were waited for; matrix products, arithmetic and copies ran while one was open for 15% of the time, Pallas kernels for 0%

commit v1 on v0

--- a/solution.py
+++ b/solution.py
@@ -274,7 +274,23 @@
         tiled=True,
     ).astype(jnp.float32)
     layer_out = (first[5] + ffn_total).astype(jnp.bfloat16)
-    cot_rows = lax.all_gather(cotangent, "tensor", axis=0, tiled=True)
+    ways, here, lap = (lax.axis_size("tensor"), lax.axis_index("tensor"), cotangent.shape[0])
+    shape = [n * ways if d == 0 else n for d, n in enumerate(cotangent.shape)]
+    full = lax.dynamic_update_slice_in_dim(
+        jnp.zeros(shape, cotangent.dtype), cotangent, here * lap, axis=0
+    )
+    going_up = going_down = cotangent
+    for far in range(1, ways // 2 + 1):
+        going_up = lax.ppermute(going_up, "tensor", [(d, (d + 1) % ways) for d in range(ways)])
+        full = lax.dynamic_update_slice_in_dim(full, going_up, (here - far) % ways * lap, axis=0)
+        if 2 * far < ways:
+            going_down = lax.ppermute(
+                going_down, "tensor", [(d, (d - 1) % ways) for d in range(ways)]
+            )
+            full = lax.dynamic_update_slice_in_dim(
+                full, going_down, (here + far) % ways * lap, axis=0
+            )
+    cot_rows = full
     again_rows, cot_rows = lax.optimization_barrier((token_rows, cot_rows))
     saved = forward_core(
         again_rows,

time: 2270 us -> 2260 us (level)
  waiting for transfers between devices: 982 us -> 957 us
    all_gather x1 -> x0, waiting for transfers between devices: 81.6 us -> none  [body(): cot_rows = lax.all_gather(cotangent, 'tensor', axis=0, tiled=True)]
    ppermute x0 -> x3, waiting for transfers between devices: none -> 56.7 us  [the longest x2 44.9 us: body(): lax.ppermute(going_up, 'tensor', [(d, (d + 1) % ways) for d in range(ways)])]
    unnamed x21 -> x20, waiting for transfers between devices: 262 us -> 261 us
    unnamed x73 -> x75, local copies, waits for them, and re-layouts: 189 us -> 189 us
  transfers between devices with their start and end apart: 16 -> 18, of which waited for: 15 -> 17; matrix products, arithmetic and copies ran while one was open for 15% -> 16% of each run, Pallas kernels for 0% -> 0%
where the time goes in v1:
time: 2260 us; the launch traced here: 2250 us
  waiting for transfers between devices  957 us (42%)
  local copies, waits for them, and re-layouts  709 us (31%)
  matrix products  407 us (18%)
  other arithmetic  139 us (6%)
    unnamed x20, waiting for transfers between devices  261 us
    unnamed x75, local copies, waits for them, and re-layouts  189 us
    reduce_scatter x2, waiting for transfers between devices, forward_core(): lax.psum_scatter(jnp.dot(context, attn_out, preferred_element_type=jnp.fl...  151 us
    while x48, local copies, waits for them, and re-layouts  135 us
    dot_general x6, matrix products, page_scores(): jnp.einsum('ihd,jhd->hij', query, key_rows, preferred_element_type=jnp.fl...  116 us
    all_gather x2, waiting for transfers between devices, forward_core(): gathered_two = lax.all_gather(normed_two, 'tensor', axis=0, tiled=True)  101 us
    all_gather x2, waiting for transfers between devices, forward_core(): gathered_one = lax.all_gather(normed_one, 'tensor', axis=0, tiled=True)  81.4 us
    all_gather x1, waiting for transfers between devices, body(): lax.all_gather(grad_resid.astype(jnp.bfloat16), 'tensor', axis=0, tiled=T...  80.9 us
  transfers between devices with their start and end apart: 18, of which 17 were waited for; matrix products, arithmetic and copies ran while one was open for 16% of the time, Pallas kernels for 0%

profile of v1, /device:TPU:0, one launch (start us, length us, event | category | flops | bytes accessed | tf_op | source)
XLA Modules:
  0.0 2254.2 jit_solution(2939728259902693589)
XLA Ops:
  12.4 24.3 %collective-permute-done = bf16[512,1024]{1,0:T(8,128)(2,1)} collective-permute-done((bf16[512,1024]{1,0:T(8,128)(2,1)}, bf16[512,1024]{1,0:T(8,128)(2,1)}, u32[]{:S(2)}, u32[]{:S(2)}) %collective-permute-start) | collective-permute-done | bytes 1048608 | tf_op jit(solution)/shard_map/ppermute | solution.py:284
  100.5 38.0 %copy.157 = f32[1,4,1024,2048]{3,1,2,0:T(4,128)} copy(f32[1,4,1024,2048]{3,2,1,0:T(8,128)} %broadcast_bitcast_fusion) | data formatting | bytes 67108864
  138.4 23.8 %slice.90 = f32[4,2096128]{1,0:T(4,128)} slice(f32[4,2097152]{1,0:T(4,128)} %bitcast.428), slice={[0:4], [0:2096128]} | slice | bytes 67076096 | tf_op jit(solution)/shard_map/slice | solution.py:58
  162.2 94.2 %reshape.284 = f32[8384512]{0:T(1024)} reshape(f32[4,2096128]{1,0:T(4,128)} %slice.90) | data formatting | bytes 67076096
  256.4 49.8 %reshape.234 = f32[4,1024,2047]{2,1,0:T(8,128)} reshape(f32[8384512]{0:T(1024)} %reshape.284) | data formatting | bytes 67076096 | tf_op jit(solution)/shard_map/reshape | solution.py:58
  370.4 108.1 %while.40 = (s32[]{:T(128)}, bf16[2,1024,256]{2,1,0:T(8,128)(2,1)}, f32[2,4,1024]{2,1,0:T(4,128)}, bf16[2,1024,4,64]{1,3,2,0:T(8,128)(2,1)}, s32[2]{0:T(128)}, /...) while((s32[]{:T(128)}, bf16[2,1024,256]{2,1,0:T(8,128)(2,1)}, ...), condition=%wide.region_12.13_spmd, body=%wide.region_9.12_spmd.sunk | while | flops 4530406400 | bytes 113618096 | solution.py:125
  483.5 75.6 %reduce-scatter.26.cloned.1.call-done = bf16[512,1024]{1,0:T(8,128)(2,1)} async-done(((bf16[2048,1024]{1,0:T(8,128)(2,1)}), bf16[512,1024]{1,0:T(8,128)(2,1)}) %reduce-scatter.26.cloned.1.call-update) | async-done | bytes 1048592 | tf_op jit(solution)/shard_map/reduce_scatter | solution.py:210
  564.4 81.4 %all-gather.12.cloned.1.call-done = bf16[2048,1024]{1,0:T(8,128)(2,1)} async-done(((bf16[512,1024]{1,0:T(8,128)(2,1)}), bf16[2048,1024]{1,0:T(8,128)(2,1)}) %all-gather.12.cloned.1.call-update) | async-done | bytes 4194320 | tf_op jit(solution)/shard_map/all_gather | solution.py:222
  675.3 75.4 %reduce-scatter.28.cloned.1.call-done = bf16[512,1024]{1,0:T(8,128)(2,1)} async-done(((bf16[2048,1024]{1,0:T(8,128)(2,1)}), bf16[512,1024]{1,0:T(8,128)(2,1)}) %reduce-scatter.28.cloned.1.call-update) | async-done | bytes 1048592 | tf_op jit(solution)/shard_map/reduce_scatter | solution.py:328
  758.6 80.9 %all-gather.14.cloned.1.call-done = bf16[2048,1024]{1,0:T(8,128)(2,1)} async-done(((bf16[512,1024]{1,0:T(8,128)(2,1)}), bf16[2048,1024]{1,0:T(8,128)(2,1)}) %all-gather.14.cloned.1.call-update) | async-done | bytes 4194320 | tf_op jit(solution)/shard_map/all_gather | solution.py:341
  852.7 531.6 %while.41 = (s32[]{:T(128)}, f32[4,2047]{1,0:T(4,128)}, f32[2,4,64,64]{2,3,1,0:T(8,128)S(1)}, bf16[2,3,1024,256]{3,2,0,1:T(8,128)(2,1)}, s32[2]{0:T(128)}, /*ind...) while((s32[]{:T(128)}, f32[4,2047]{1,0:T(4,128)}, ...), condition=%wide.region_20.21_spmd.clone, body=%wide.region_17.20_spmd.clone.sunk | while | flops 9586938880 | bytes 645969984 | solution.py:171
  985.8 46.4 %reshape.288 = f32[8384512]{0:T(1024)} reshape(f32[4,1024,2047]{2,1,0:T(8,128)} %pad.19.clone.2) | data formatting | bytes 67076096 | tf_op jit(solution)/shard_map/while
  1032.3 40.4 %reshape.289 = f32[4,2096128]{1,0:T(4,128)} reshape(f32[8384512]{0:T(1024)} %reshape.288) | data formatting | bytes 67076096 | tf_op jit(solution)/shard_map/while/body/eval_jaxpr/reshape | solution.py:65
  1248.6 46.2 %reshape.288 = f32[8384512]{0:T(1024)} reshape(f32[4,1024,2047]{2,1,0:T(8,128)} %pad.19.clone.2) | data formatting | bytes 67076096 | tf_op jit(solution)/shard_map/while
  1294.8 40.4 %reshape.289 = f32[4,2096128]{1,0:T(4,128)} reshape(f32[8384512]{0:T(1024)} %reshape.288) | data formatting | bytes 67076096 | tf_op jit(solution)/shard_map/while/body/eval_jaxpr/reshape | solution.py:65
  1392.3 75.4 %reduce-scatter.30.cloned.1.call-done = bf16[512,1024]{1,0:T(8,128)(2,1)} async-done(((bf16[2048,1024]{1,0:T(8,128)(2,1)}), bf16[512,1024]{1,0:T(8,128)(2,1)}) %reduce-scatter.30.cloned.1.call-update) | async-done | bytes 1048592 | tf_op jit(solution)/shard_map/reduce_scatter | solution.py:353
  1475.6 81.4 %all-gather.6.cloned.1.call-done = bf16[2048,1024]{1,0:T(8,128)(2,1)} async-done(((bf16[512,1024]{1,0:T(8,128)(2,1)}), bf16[2048,1024]{1,0:T(8,128)(2,1)}) %all-gather.6.cloned.1.call-update) | async-done | bytes 4194320 | tf_op jit(solution)/shard_map/all_gather | solution.py:205
  1591.6 106.5 %while.39 = (s32[]{:T(128)}, bf16[2,1024,256]{2,1,0:T(8,128)(2,1)}, bf16[2,1024,4,64]{1,3,2,0:T(8,128)(2,1)}, s32[2]{0:T(128)}, bf16[2,1024,4,64]{1,3,2,0:T(8,12...) while((s32[]{:T(128)}, bf16[2,1024,256]{2,1,0:T(8,128)(2,1)}, ...), condition=%wide.region_4.5_spmd, body=%wide.region_1.4_spmd.sunk | while | flops 4530390016 | bytes 113568936 | solution.py:125
  1703.3 75.0 %reduce-scatter.22.cloned.1.call-done = bf16[512,1024]{1,0:T(8,128)(2,1)} async-done(((bf16[2048,1024]{1,0:T(8,128)(2,1)}), bf16[512,1024]{1,0:T(8,128)(2,1)}) %reduce-scatter.22.cloned.1.call-update) | async-done | bytes 1048592 | tf_op jit(solution)/shard_map/reduce_scatter | solution.py:210
  1880.2 24.5 %reduce-scatter.40.cloned.1.call-done = bf16[128,704]{1,0:T(8,128)(2,1)} async-done(((bf16[1024,704]{1,0:T(8,128)(2,1)}), bf16[128,704]{1,0:T(8,128)(2,1)}) %reduce-scatter.40.cloned.1.call-update) | async-done | bytes 180240
  1906.6 46.4 %reduce-scatter.38.cloned.1.call-done = bf16[128,1408]{1,0:T(8,128)(2,1)} async-done(((bf16[1024,1408]{1,0:T(8,128)(2,1)}), bf16[128,1408]{1,0:T(8,128)(2,1)}) %reduce-scatter.38.cloned.1.call-update) | async-done | bytes 360464
  1992.0 40.1 %reduce-scatter.34.cloned.1.call-done = bf16[128,768]{1,0:T(8,128)(2,1)} async-done(((bf16[1024,768]{1,0:T(8,128)(2,1)}), bf16[128,768]{1,0:T(8,128)(2,1)}) %reduce-scatter.34.cloned.1.call-update) | async-done | bytes 196624
  2034.3 134.1 %reduce-scatter.32.cloned.1.call-done = f32[32,2]{1,0:T(8,128)} async-done(((f32[1024,2]{1,0:T(8,128)}), f32[32,2]{1,0:T(8,128)}) %reduce-scatter.32.cloned.1.call-update) | async-done | bytes 272
  2169.7 74.4 %reduce-scatter.24.cloned.1.call-done = bf16[512,1024]{1,0:T(8,128)(2,1)} async-done(((bf16[2048,1024]{1,0:T(8,128)(2,1)}), bf16[512,1024]{1,0:T(8,128)(2,1)}) %reduce-scatter.24.cloned.1.call-update) | async-done | bytes 1048592 | tf_op jit(solution)/shard_map/reduce_scatter | solution.py:267
  (332 shorter events, 963.5 us)
Async XLA Ops:
  7.2 638.6 %copy-start = (bf16[2,1024,704]{1,2,0:T(8,128)(2,1)S(1)}, bf16[2,1024,704]{1,2,0:T(8,128)(2,1)}, u32[]{:S(2)}) copy-start(bf16[2,1024,704]{1,2,0:T(8,128)(2,1)} %param.24) | copy-start | bytes 8650756
  7.2 328.8 %all-gather.10.cloned.1.call-start = ((), (), s32[]{:S(2)}) async-start(), calls=%async_computation.14 | async-start | bytes 5242880 | tf_op jit(solution)/shard_map/all_gather | solution.py:205
  7.2 29.5 %collective-permute-start = (bf16[512,1024]{1,0:T(8,128)(2,1)}, bf16[512,1024]{1,0:T(8,128)(2,1)}, u32[]{:S(2)}, u32[]{:S(2)}) collective-permute-start(bf16[512,1024]{1,0:T(8,128)(2,1)} %param.29), channel_id=1, source_target_pairs={{0,1},{1,2},{2,3},{3,0},{4,5},{5,6},{6,7},{7,4},{8,9},{9,10},{10,1... | collective-permute-start | bytes 3145736 | tf_op jit(solution)/shard_map/ppermute | solution.py:284
  10.3 47.6 %collective-permute-start.1 = (bf16[512,1024]{1,0:T(8,128)(2,1)}, bf16[512,1024]{1,0:T(8,128)(2,1)}, u32[]{:S(2)}, u32[]{:S(2)}) collective-permute-start(bf16[512,1024]{1,0:T(8,128)(2,1)} %param.29), channel_id=1, source_target_pairs={{0,3},{1,0},{2,1},{3,2},{4,7},{5,4},{6,5},{7,6},{8,11},{9,8},{10,9... | collective-permute-start | bytes 3145736 | tf_op jit(solution)/shard_map/ppermute | solution.py:287
  36.7 44.1 %collective-permute-start.2 = (bf16[512,1024]{1,0:T(8,128)(2,1)}, bf16[512,1024]{1,0:T(8,128)(2,1)}, u32[]{:S(2)}, u32[]{:S(2)}) collective-permute-start(bf16[512,1024]{1,0:T(8,128)(2,1)} %collective-permute-done), channel_id=1, source_target_pairs={{0,1},{1,2},{2,3},{3,0},{4,5},{5,6},{6,7},{7,4},{8,9},{9,10},{10,1... | collective-permute-start | bytes 3145736 | tf_op jit(solution)/shard_map/ppermute | solution.py:284
  85.7 473.5 %reduce-scatter.26.cloned.1.call-start = ((), (), s32[]{:S(2)}) async-start(), calls=%async_computation.15 | async-start | bytes 5242880 | tf_op jit(solution)/shard_map/reduce_scatter | solution.py:210
  483.3 78.3 %copy-start.21 = (f32[1,1024]{1,0:T(1,128)S(1)}, f32[1,1024]{1,0:T(1,128)}, u32[]{:S(2)}) copy-start(f32[1,1024]{1,0:T(1,128)} %get-tuple-element.536) | copy-start | bytes 12292
  483.3 162.5 %all-gather.12.cloned.1.call-start = ((), (), s32[]{:S(2)}) async-start(), calls=%async_computation.16 | async-start | bytes 5242880 | tf_op jit(solution)/shard_map/all_gather | solution.py:222
  564.3 186.4 %reduce-scatter.28.cloned.1.call-start = ((), (), s32[]{:S(2)}) async-start(), calls=%async_computation.17 | async-start | bytes 5242880 | tf_op jit(solution)/shard_map/reduce_scatter | solution.py:328
  675.2 164.3 %all-gather.14.cloned.1.call-start = ((), (), s32[]{:S(2)}) async-start(), calls=%async_computation.18 | async-start | bytes 5242880 | tf_op jit(solution)/shard_map/all_gather | solution.py:341
  758.2 709.5 %reduce-scatter.30.cloned.1.call-start = ((), (), s32[]{:S(2)}) async-start(), calls=%async_computation.19 | async-start | bytes 5242880 | tf_op jit(solution)/shard_map/reduce_scatter | solution.py:353
  1392.2 75.5 %copy-start.26 = (f32[512]{0:T(512)S(1)}, f32[512]{0:T(512)}, u32[]{:S(2)}) copy-start(f32[512]{0:T(512)} %copy-done.25) | copy-start | bytes 6148
  1392.2 78.6 %copy-start.30 = (f32[512]{0:T(512)S(1)}, f32[512]{0:T(512)}, u32[]{:S(2)}) copy-start(f32[512]{0:T(512)} %get-tuple-element.538) | copy-start | bytes 6148
  1392.3 164.7 %all-gather.6.cloned.1.call-start = ((), (), s32[]{:S(2)}) async-start(), calls=%async_computation.10 | async-start | bytes 5242880 | tf_op jit(solution)/shard_map/all_gather | solution.py:205
  1475.5 302.8 %reduce-scatter.22.cloned.1.call-start = ((), (), s32[]{:S(2)}) async-start(), calls=%async_computation.11 | async-start | bytes 5242880 | tf_op jit(solution)/shard_map/reduce_scatter | solution.py:210
  1702.8 77.4 %copy-start.22 = (f32[1,1024]{1,0:T(1,128)S(1)}, f32[1,1024]{1,0:T(1,128)}, u32[]{:S(2)}) copy-start(f32[1,1024]{1,0:T(1,128)} %get-tuple-element.536) | copy-start | bytes 12292
  1702.8 161.8 %all-gather.8.cloned.1.call-start = ((), (), s32[]{:S(2)}) async-start(), calls=%async_computation.12 | async-start | bytes 5242880 | tf_op jit(solution)/shard_map/all_gather | solution.py:222
  1783.2 121.6 %reduce-scatter.40.cloned.1.call-start = ((), (), s32[]{:S(2)}) async-start(), calls=%async_computation.24 | async-start | bytes 1769472
  1796.4 156.6 %reduce-scatter.38.cloned.1.call-start = ((), (), s32[]{:S(2)}) async-start(), calls=%async_computation.23 | async-start | bytes 3244032
  1823.3 167.1 %reduce-scatter.36.cloned.1.call-start = ((), (), s32[]{:S(2)}) async-start(), calls=%async_computation.22 | async-start | bytes 589824
  1828.2 203.9 %reduce-scatter.34.cloned.1.call-start = ((), (), s32[]{:S(2)}) async-start(), calls=%async_computation.21 | async-start | bytes 1769472
  1843.5 324.8 %reduce-scatter.32.cloned.1.call-start = ((), (), s32[]{:S(2)}) async-start(), calls=%async_computation.20 | async-start | bytes 540672
  1844.7 399.4 %reduce-scatter.24.cloned.1.call-start = ((), (), s32[]{:S(2)}) async-start(), calls=%async_computation.13 | async-start | bytes 5242880 | tf_op jit(solution)/shard_map/reduce_scatter | solution.py:267
  1878.3 79.1 %copy-start.15 = (f32[2,4,64,64]{2,3,1,0:T(8,128)S(1)}, f32[2,4,64,64]{2,3,1,0:T(8,128)}, u32[]{:S(2)}) copy-start(f32[2,4,64,64]{2,3,1,0:T(8,128)} %copy-done.14) | copy-start | bytes 393220
  (43 other events, 506.9 us)
Sparse Core Ops, SparseCore 0:
  85.8 80.1 all-gather.9
  483.4 75.7 reduce-scatter.25
  564.4 81.2 all-gather.11
  675.4 75.2 reduce-scatter.27
  758.3 81.2 all-gather.13
  1392.4 75.2 reduce-scatter.29
  1475.6 81.2 all-gather.5
  1702.9 75.2 reduce-scatter.21
  1783.3 81.2 all-gather.7
  1867.7 36.9 reduce-scatter.39
  1908.1 44.8 reduce-scatter.37
  1956.2 34.1 reduce-scatter.35
  1993.7 38.4 reduce-scatter.33
  2034.3 134.0 reduce-scatter.31
  2170.6 73.4 reduce-scatter.23
